TPU v7x, 32 devices: a whole 2x2x4 slice. The times are simulated.
32 devices in a mesh: dp: 8 (over z, y), mp: 4 (over x, core).
Axes of the slice: x: 2, y: 2, z: 4, core: 2. Of those that a mesh axis runs over, the one named last changes fastest.
Arguments:
- hidden: bfloat16 [16, 64, 3584], P('dp', None, 'mp'), may hold values from -6 to 6
- rewards: float32 [16, 64], P('dp'), may hold values from -6 to 6
- actions: int32 [16, 64], P('dp'), may hold values from 0 to 152063, as said below
- lengths: int32 [16], P('dp'), may hold values from 1 to 64, 512 in all
- table: bfloat16 [152064, 3584], P('dp', 'mp'), may hold values from -0.09375 to 0.09375
- q_one: bfloat16 [3584, 3584], P('dp', 'mp'), may hold values from -0.09375 to 0.09375
- q_two: bfloat16 [3584, 3584], P('dp', 'mp'), may hold values from -0.09375 to 0.09375
- t_one: bfloat16 [3584, 3584], P('dp', 'mp'), may hold values from -0.09375 to 0.09375
- t_two: bfloat16 [3584, 3584], P('dp', 'mp'), may hold values from -0.09375 to 0.09375
- value_weight: bfloat16 [3584], P('mp'), may hold values from -0.09375 to 0.09375
- value_bias: float32 [1], replicated, may hold values from -3 to 3
Outputs:
- loss: float32 [], replicated
- grad_q_one: float32 [3584, 3584], P('dp', 'mp')
- grad_q_two: float32 [3584, 3584], P('dp', 'mp')
- grad_value: float32 [3584], P('mp')
- grad_bias: float32 [1], replicated
- target_one: bfloat16 [3584, 3584], P('dp', 'mp')
- target_two: bfloat16 [3584, 3584], P('dp', 'mp')
Inputs may be any that keep to these rules, and one draw needn't show every extreme that they name: `actions`: among the 128 positions of the prompts of one index of dp, exactly 16 action ids fall in each of the aligned blocks of 19008 vocabulary rows.
All inputs are finite; a program needn't handle non-finite values. No bound on the sum of `lengths` on one device may be relied on, other than what follows from the above.
Results may differ from a plain program's by a relative error of at most 0.0045.
Values may be sent and summed in bfloat16 or wider, within the bound.
A program may use at most 192 MiB of HBM per device.

v0:
```python
import jax
import jax.numpy as jnp
from jax import lax
from jax.sharding import PartitionSpec as P

discount = 0.99
expectile = 0.7
polyak_rate = 0.005


def head_gelu(inputs):
    return jax.nn.gelu(inputs, approximate=True)


def slope(preact, upstream):
    _, pullback = jax.vjp(head_gelu, preact)
    return pullback(upstream)[0]


def critic_terms(q_first, q_second, t_first, t_second, values, rewards, lengths):
    positions = jnp.arange(values.shape[1], dtype=jnp.int32)[None, :]
    valid = positions < lengths[:, None]
    follows = positions + 1 < lengths[:, None]
    shifted = jnp.concatenate([values[:, 1:], jnp.zeros_like(values[:, :1])], axis=1)
    target = rewards + discount * jnp.where(follows, shifted, 0.0)
    lowest = jnp.minimum(t_first, t_second)
    spread = lowest - values
    weights = jnp.where(spread < 0.0, 1.0 - expectile, expectile)
    err_one = q_first - target
    err_two = q_second - target
    loss_sum = jnp.sum(
        jnp.where(valid, err_one * err_one + err_two * err_two + weights * spread * spread, 0.0)
    )
    grad_first = jnp.where(valid, 2.0 * err_one, 0.0)
    grad_second = jnp.where(valid, 2.0 * err_two, 0.0)
    grad_values = jnp.where(valid, -2.0 * weights * spread, 0.0)
    return (grad_first, grad_second, grad_values, loss_sum)


def lookup(wanted_ids, table):
    holders_count = lax.axis_size("dp")
    local_rows = table.shape[0]
    id_count = wanted_ids.shape[0]
    per_holder = id_count // holders_count
    holders = wanted_ids // local_rows
    ranking = jnp.argsort(holders * id_count + jnp.arange(id_count, dtype=jnp.int32))
    requests = (wanted_ids % local_rows)[ranking].reshape(holders_count, per_holder)
    found = table[lax.all_to_all(requests, "dp", split_axis=0, concat_axis=0, tiled=True)]
    fetched = lax.all_to_all(found, "dp", split_axis=0, concat_axis=0, tiled=True)
    inverse = jnp.argsort(ranking)
    return fetched.reshape(id_count, -1)[inverse]


def on_device(
    hidden, rewards, actions, lengths, table, q_one, q_two, t_one, t_two, value_weight, value_bias
):
    prompt_count, slot_count, local_width = hidden.shape
    positions_count = prompt_count * slot_count
    gathered = lax.all_gather(hidden, "mp", axis=2, tiled=True)
    flat = gathered.reshape(positions_count, -1)
    local_flat = hidden.reshape(positions_count, local_width)
    embed = lookup(actions.reshape(positions_count), table).astype(jnp.float32)
    head_cols = q_one.shape[1]

    def add_rows(pieces):
        return tuple((jnp.dot(flat, piece, preferred_element_type=jnp.float32) for piece in pieces))

    preacts = add_rows(
        (
            lax.all_gather(q_one, "dp", axis=0, tiled=True),
            lax.all_gather(q_two, "dp", axis=0, tiled=True),
            lax.all_gather(t_one, "dp", axis=0, tiled=True),
            lax.all_gather(t_two, "dp", axis=0, tiled=True),
        )
    )
    partial_value = [jnp.sum(head_gelu(preact) * embed, axis=1) for preact in preacts]
    value_part = jnp.dot(local_flat, value_weight, preferred_element_type=jnp.float32)
    summed = lax.psum(
        (partial_value[0], partial_value[1], partial_value[2], partial_value[3], value_part), "mp"
    )
    shaped = [piece.reshape(prompt_count, slot_count) for piece in summed]
    values = shaped[4] + value_bias[0]
    grad_first, grad_second, grad_values, loss_sum = critic_terms(
        shaped[0], shaped[1], shaped[2], shaped[3], values, rewards, lengths
    )
    back_one = slope(preacts[0], grad_first.reshape(-1, 1) * embed).astype(jnp.bfloat16)
    back_two = slope(preacts[1], grad_second.reshape(-1, 1) * embed).astype(jnp.bfloat16)
    local_count = jnp.sum(lengths).astype(jnp.float32)
    holders_count = lax.axis_size("dp")
    row_share = q_one.shape[0]
    dims = (((0,), (0,)), ((), ()))
    total_count = lax.psum(local_count, "dp")
    factor = 1.0 / total_count
    term_one = (
        lax.dot_general(flat, back_one, dims, preferred_element_type=jnp.float32) * factor
    ).reshape(holders_count, row_share, head_cols)
    term_two = (
        lax.dot_general(flat, back_two, dims, preferred_element_type=jnp.float32) * factor
    ).reshape(holders_count, row_share, head_cols)
    head_one = jnp.sum(
        lax.all_to_all(term_one, "dp", split_axis=0, concat_axis=0, tiled=True), axis=0
    )
    head_two = jnp.sum(
        lax.all_to_all(term_two, "dp", split_axis=0, concat_axis=0, tiled=True), axis=0
    )
    value_part_grad = jnp.dot(
        grad_values.reshape(-1), local_flat.astype(jnp.float32), precision=lax.Precision.HIGHEST
    )
    bias_part = jnp.sum(grad_values)
    value_grad, bias_grad, loss_total = lax.psum(
        (value_part_grad * factor, bias_part * factor, loss_sum * factor), "dp"
    )
    new_one = (
        (1.0 - polyak_rate) * t_one.astype(jnp.float32) + polyak_rate * q_one.astype(jnp.float32)
    ).astype(jnp.bfloat16)
    new_two = (
        (1.0 - polyak_rate) * t_two.astype(jnp.float32) + polyak_rate * q_two.astype(jnp.float32)
    ).astype(jnp.bfloat16)
    return (loss_total, head_one, head_two, value_grad, bias_grad.reshape(1), new_one, new_two)


def solution(mesh):
    in_specs = (
        P("dp", None, "mp"),
        P("dp", None),
        P("dp", None),
        P("dp"),
        P("dp", "mp"),
        P("dp", "mp"),
        P("dp", "mp"),
        P("dp", "mp"),
        P("dp", "mp"),
        P("mp"),
        P(),
    )
    out_specs = (P(), P("dp", "mp"), P("dp", "mp"), P("mp"), P(), P("dp", "mp"), P("dp", "mp"))
    return jax.shard_map(
        on_device, mesh=mesh, in_specs=in_specs, out_specs=out_specs, check_vma=False
    )
```

profile of v0, /device:TPU:16, one launch (start us, length us, event | category | flops | bytes accessed | tf_op | source)
XLA Modules:
  0.0 1046.5 jit_solution(4205179410584467685)
XLA Ops:
  11.6 2.5 sort.31
  14.2 1.2 gather_fusion
  16.1 6.2 all-to-all-start
  22.2 2.5 sort.32
  25.5 1.3 reduce_sum.86
  27.4 1.1 convolution_bitcast_fusion
  29.3 17.2 %psum.68 = f32[]{:T(128)} all-reduce(f32[]{:T(128)S(6)} %convert_element_type.32), channel_id=1, replica_groups=mesh['dp'=8,'mp'=4] {'dp'}, use_global_device_ids=true, to_apply=%region_13.14 | all-reduce | flops 1 | bytes 8 | tf_op jit(solution)/shard_map/psum | solution.py:92
  48.0 2.9 gather_fusion.1
  50.9 9.7 all-to-all-start.1
  60.7 9.1 all_gather.15
  69.8 1.5 all-to-all-done.1
  72.2 41.4 %all-gather.7.cloned.1.call-done = bf16[3584,896]{1,0:T(8,128)(2,1)} async-done(((bf16[448,896]{1,0:T(8,128)(2,1)}), bf16[3584,896]{1,0:T(8,128)(2,1)}) %all-gather.7.cloned.1.call-update) | async-done | bytes 6422544 | tf_op jit(solution)/shard_map/all_gather | solution.py:71
  113.6 3.9 fusion.83
  117.5 97.8 %all-gather.9.cloned.1.call-done = bf16[3584,896]{1,0:T(8,128)(2,1)} async-done(((bf16[448,896]{1,0:T(8,128)(2,1)}), bf16[3584,896]{1,0:T(8,128)(2,1)}) %all-gather.9.cloned.1.call-update) | async-done | bytes 6422544 | tf_op jit(solution)/shard_map/all_gather | solution.py:72
  215.3 3.9 fusion.84
  219.3 96.7 %all-gather.11.cloned.1.call-done = bf16[3584,896]{1,0:T(8,128)(2,1)} async-done(((bf16[448,896]{1,0:T(8,128)(2,1)}), bf16[3584,896]{1,0:T(8,128)(2,1)}) %all-gather.11.cloned.1.call-update) | async-done | bytes 6422544 | tf_op jit(solution)/shard_map/all_gather | solution.py:73
  316.0 3.9 fusion.85
  320.0 96.6 %all-gather.5.cloned.1.call-done = bf16[3584,896]{1,0:T(8,128)(2,1)} async-done(((bf16[448,896]{1,0:T(8,128)(2,1)}), bf16[3584,896]{1,0:T(8,128)(2,1)}) %all-gather.5.cloned.1.call-update) | async-done | bytes 6422544 | tf_op jit(solution)/shard_map/all_gather | solution.py:70
  416.6 4.5 fusion.38
  421.3 5.8 all-reduce.2
  428.0 6.7 multiply_bitcast_fusion
  434.7 14.2 %copy.22 = f32[3584,896]{1,0:T(8,128)} copy(f32[3584,896]{0,1:T(8,128)} %multiply_bitcast_fusion) | data formatting | bytes 25690112 | tf_op jit(solution)/shard_map/mul | solution.py:98
  448.9 6.5 all-to-all-start.3
  456.3 6.7 multiply_bitcast_fusion.1
  463.0 14.1 %copy.21 = f32[3584,896]{1,0:T(8,128)} copy(f32[3584,896]{0,1:T(8,128)} %multiply_bitcast_fusion.1) | data formatting | bytes 25690112 | tf_op jit(solution)/shard_map/mul | solution.py:95
  477.1 253.9 %all-to-all-done.3 = f32[8,448,896]{2,1,0:T(8,128)} async-done(((f32[8,448,896]{2,1,0:T(8,128)}), f32[8,448,896]{2,1,0:T(8,128)}, u32[]{:S(2)}, u32[]{:S(2)}) %all-to-all-start.3) | async-done | bytes 12845088 | tf_op jit(solution)/shard_map/all_to_all | solution.py:104
  731.0 8.9 all-to-all-start.2
  740.0 1.2 add_convert_fusion
  741.2 1.2 add_convert_fusion.1
  744.0 282.8 %all-reduce.1 = (f32[]{:T(128)}, f32[896]{0:T(1024)}, f32[1]{0:T(128)}) all-reduce(f32[]{:T(128)S(6)} %mul.253, f32[896]{0:T(1024)S(1)} %broadcast_multiply_fusion, f32[1]{0:T(128)} %bitcast.14), channel_id=1, replica_groups=mesh['dp'=8,'mp'=4] {'dp'}, use_global_device_ids=true, to_apply=%region_14.15 | all-reduce | flops 898 | bytes 7184 | tf_op jit(solution)/shard_map/psum | solution.py:110
  1026.8 6.6 reduce_sum.88
  1033.4 6.6 reduce_sum.87
  (57 shorter events, 9.8 us)
Async XLA Ops:
  7.2 53.5 %copy-start.4 = (bf16[2,64,896]{2,1,0:T(8,128)(2,1)S(1)}, bf16[2,64,896]{2,1,0:T(8,128)(2,1)}, u32[]{:S(2)}) copy-start(bf16[2,64,896]{2,1,0:T(8,128)(2,1)} %param.11) | copy-start | bytes 688132
  7.2 106.4 %all-gather.7.cloned.1.call-start = ((), (), s32[]{:S(2)}) async-start(), calls=%async_computation.5 | async-start | bytes 7225344 | tf_op jit(solution)/shard_map/all_gather | solution.py:71
  7.9 207.4 %all-gather.9.cloned.1.call-start = ((), (), s32[]{:S(2)}) async-start(), calls=%async_computation.6 | async-start | bytes 7225344 | tf_op jit(solution)/shard_map/all_gather | solution.py:72
  8.7 307.4 %all-gather.11.cloned.1.call-start = ((), (), s32[]{:S(2)}) async-start(), calls=%async_computation.7 | async-start | bytes 7225344 | tf_op jit(solution)/shard_map/all_gather | solution.py:73
  9.4 407.2 %all-gather.5.cloned.1.call-start = ((), (), s32[]{:S(2)}) async-start(), calls=%async_computation.4 | async-start | bytes 7225344 | tf_op jit(solution)/shard_map/all_gather | solution.py:70
  16.1 31.8 %all-to-all-start = ((s32[8,1,16]{2,1,0:T(1,128)}), s32[8,1,16]{2,1,0:T(1,128)S(1)}, u32[]{:S(2)}, u32[]{:S(2)}) async-start(s32[8,1,16]{2,1,0:T(1,128)} %bitcast.1), calls=%async_computation | async-start | bytes 8192 | tf_op jit(solution)/shard_map/all_to_all | solution.py:48
  50.9 20.4 %all-to-all-start.1 = ((bf16[8,16,896]{2,1,0:T(8,128)(2,1)}), bf16[8,16,896]{2,1,0:T(8,128)(2,1)S(1)}, u32[]{:S(2)}, u32[]{:S(2)}) async-start(bf16[8,16,896]{2,1,0:T(8,128)(2,1)} %bitcast.3), calls=%async_computation.1 | async-start | bytes 458752 | tf_op jit(solution)/shard_map/all_to_all | solution.py:49
  320.0 107.8 %copy-start.5 = (s32[2]{0:T(128)S(1)}, s32[2]{0:T(128)}, u32[]{:S(2)}) copy-start(s32[2]{0:T(128)} %param.14) | copy-start | bytes 28
  320.0 107.8 %copy-start.6 = (f32[2,64]{1,0:T(2,128)S(1)}, f32[2,64]{1,0:T(2,128)}, u32[]{:S(2)}) copy-start(f32[2,64]{1,0:T(2,128)} %param.12) | copy-start | bytes 1540
  448.9 282.1 %all-to-all-start.3 = ((f32[8,448,896]{2,1,0:T(8,128)}), f32[8,448,896]{2,1,0:T(8,128)}, u32[]{:S(2)}, u32[]{:S(2)}) async-start(f32[8,448,896]{2,1,0:T(8,128)} %bitcast.37), calls=%async_computation.3 | async-start | bytes 25690112 | tf_op jit(solution)/shard_map/all_to_all | solution.py:104
  731.0 9.0 copy-start
  731.0 9.0 copy-start.1
  731.0 10.1 copy-start.2
  731.0 10.1 copy-start.3
  731.0 302.4 %all-to-all-start.2 = ((f32[8,448,896]{2,1,0:T(8,128)}), f32[8,448,896]{2,1,0:T(8,128)}, u32[]{:S(2)}, u32[]{:S(2)}) async-start(f32[8,448,896]{2,1,0:T(8,128)} %bitcast.36), calls=%async_computation.2 | async-start | bytes 25690112 | tf_op jit(solution)/shard_map/all_to_all | solution.py:101
Sparse Core Ops, SparseCore 0:
  10.2 103.3 all-gather.6
  115.7 99.5 all-gather.8
  217.5 98.4 all-gather.10
  318.1 98.4 all-gather.4
where the time goes:
time: 1050 us
  waiting for transfers between devices  591 us (56%)
  blocking collectives  315 us (30%)
  local copies, waits for them, and re-layouts  35.7 us (3%)
  starting transfers between devices  31.5 us (3%)
  matrix products  31.2 us (3%)
  other arithmetic  25.5 us (2%)
  between operations  17.2 us (2%)
    psum x1, blocking collectives, on_device(): lax.psum((value_part_grad * factor, bias_part * factor, loss_sum * factor...  283 us
    all_to_all x1, waiting for transfers between devices, on_device(): lax.all_to_all(term_two, 'dp', split_axis=0, concat_axis=0, tiled=True)  254 us
    all_gather x1, waiting for transfers between devices, on_device(): lax.all_gather(t_one, 'dp', axis=0, tiled=True)  97.8 us
    all_gather x1, waiting for transfers between devices, on_device(): lax.all_gather(t_two, 'dp', axis=0, tiled=True)  96.7 us
    all_gather x1, waiting for transfers between devices, on_device(): lax.all_gather(q_one, 'dp', axis=0, tiled=True)  96.6 us
    all_gather x1, waiting for transfers between devices, on_device(): lax.all_gather(q_two, 'dp', axis=0, tiled=True)  41.4 us
  transfers between devices with their start and end apart: 8, of which 6 were waited for; matrix products, arithmetic and copies ran while one was open for 6% of the time, Pallas kernels for 0%

commit v1 on v0

v1 whole, which is shorter than its diff:
```python
import jax
import jax.numpy as jnp
from jax import lax
from jax.sharding import PartitionSpec as P

discount = 0.99
expectile = 0.7
polyak_rate = 0.005
f32 = jnp.float32
bf16 = jnp.bfloat16


def head_gelu(inputs):
    return jax.nn.gelu(inputs, approximate=True)


def slope(preact, upstream):
    _, pullback = jax.vjp(head_gelu, preact)
    return pullback(upstream)[0]


def pick(mask, row):
    return jnp.sum(jnp.where(mask, row[None, :], jnp.zeros((), row.dtype)), axis=1)


def on_device(
    hidden, rewards, actions, lengths, table, q_one, q_two, t_one, t_two, value_weight, value_bias
):
    dp = lax.axis_size("dp")
    me = lax.axis_index("dp")
    prompts, slots, width = hidden.shape
    own = prompts * slots
    total = own * dp
    packed = total // 2
    share = packed // dp
    cols = q_one.shape[1]
    rows = q_one.shape[0]
    local_rows = table.shape[0]
    local_flat = hidden.reshape(own, width)

    stacked = jnp.concatenate([local_flat, value_weight.reshape(1, width)], axis=0)
    wide = lax.all_gather(stacked, "mp", axis=1, tiled=True)
    flat, value_row = wide[:own], wide[own:]
    values = (
        jnp.sum(flat.astype(f32) * value_row.astype(f32), axis=1).reshape(prompts, slots)
        + value_bias[0]
    )
    positions = jnp.arange(slots, dtype=jnp.int32)[None, :]
    follows = positions + 1 < lengths[:, None]
    shifted = jnp.concatenate([values[:, 1:], jnp.zeros_like(values[:, :1])], axis=1)
    target = rewards + discount * jnp.where(follows, shifted, 0.0)

    ints = jnp.concatenate([actions, lengths[:, None]], axis=1)
    all_ints = lax.all_gather(ints, "dp", axis=0, tiled=True)
    all_lengths = all_ints[:, slots]
    ids = all_ints[:, :slots].reshape(total)
    facts = jnp.stack([target.reshape(own), values.reshape(own)])
    all_facts = lax.all_gather(facts, "dp", axis=1, tiled=True)
    count = jnp.sum(all_lengths).astype(f32)
    factor = 1.0 / count

    prompt_ids = jnp.arange(prompts * dp, dtype=jnp.int32)
    offsets = jnp.sum(
        jnp.where(prompt_ids[None, :] < prompt_ids[:, None], all_lengths[None, :], 0), axis=1
    )
    place = jnp.where(
        positions < all_lengths[:, None], offsets[:, None] + positions, -1
    ).reshape(total)
    own_slots = jnp.arange(share, dtype=jnp.int32)[:, None] + me * share
    own_mask = own_slots == place[None, :]

    holders = ids // local_rows
    by_source = holders.reshape(dp, own)
    order = jnp.arange(own, dtype=jnp.int32)
    earlier = (by_source[:, :, None] == by_source[:, None, :]) & (
        order[None, None, :] < order[None, :, None]
    )
    per_source = own // dp
    rank = (
        jnp.sum(earlier.astype(jnp.int32), axis=2)
        + jnp.arange(dp, dtype=jnp.int32)[:, None] * per_source
    ).reshape(total)
    where_held = holders * own + rank
    wanted = jnp.arange(own, dtype=jnp.int32)[:, None] + me * own == where_held[None, :]
    requests = pick(wanted, ids - me * local_rows)
    found = table[requests]
    all_found = lax.all_gather(found, "dp", axis=0, tiled=True)
    seat = pick(own_mask, where_held)
    seat_mask = (jnp.arange(total, dtype=jnp.int32)[None, :] == seat[:, None]).astype(bf16)
    embed = jnp.dot(seat_mask, all_found, preferred_element_type=f32)

    spread = lax.all_to_all(flat, "dp", split_axis=1, concat_axis=0, tiled=True)
    pack_mask = (jnp.arange(packed, dtype=jnp.int32)[:, None] == place[None, :]).astype(bf16)
    held = jnp.dot(pack_mask, spread, preferred_element_type=f32).astype(bf16)

    partial = jnp.concatenate(
        [
            jnp.dot(held, weight, preferred_element_type=f32).astype(bf16)
            for weight in (q_one, q_two, t_one, t_two)
        ],
        axis=1,
    )
    swapped = lax.all_to_all(partial, "dp", split_axis=0, concat_axis=0, tiled=True)
    pre = jnp.sum(swapped.reshape(dp, share, 4 * cols).astype(f32), axis=0)
    pres = [pre[:, k * cols : (k + 1) * cols] for k in range(4)]
    scores = jnp.stack([jnp.sum(head_gelu(p) * embed, axis=1) for p in pres])
    board = lax.dynamic_update_slice(
        jnp.zeros((4, packed), f32), scores, (jnp.zeros((), jnp.int32), me * share)
    )
    all_scores = lax.psum(board, ("dp", "mp"))

    pack_bool = jnp.arange(packed, dtype=jnp.int32)[:, None] == place[None, :]
    goal = pick(pack_bool, all_facts[0])
    worth = pick(pack_bool, all_facts[1])
    lowest = jnp.minimum(all_scores[2], all_scores[3])
    spread_to = lowest - worth
    weights = jnp.where(spread_to < 0.0, 1.0 - expectile, expectile)
    err_one = all_scores[0] - goal
    err_two = all_scores[1] - goal
    loss = (
        jnp.sum(err_one * err_one + err_two * err_two + weights * spread_to * spread_to) * factor
    )
    grad_values = -2.0 * weights * spread_to
    bias_grad = jnp.sum(grad_values) * factor

    up_one = lax.dynamic_slice(2.0 * err_one, (me * share,), (share,))
    up_two = lax.dynamic_slice(2.0 * err_two, (me * share,), (share,))
    back = jnp.concatenate(
        [
            slope(pres[0], up_one[:, None] * embed).astype(bf16),
            slope(pres[1], up_two[:, None] * embed).astype(bf16),
        ],
        axis=1,
    )
    all_back = lax.all_gather(back, "dp", axis=0, tiled=True)
    dims = (((0,), (0,)), ((), ()))
    head_one = (
        lax.dot_general(held, all_back[:, :cols], dims, preferred_element_type=f32) * factor
    )
    head_two = (
        lax.dot_general(held, all_back[:, cols:], dims, preferred_element_type=f32) * factor
    )

    own_place = lax.dynamic_slice(place, (me * own,), (own,))
    own_errors = pick(
        own_place[:, None] == jnp.arange(packed, dtype=jnp.int32)[None, :], grad_values
    )
    value_part = jnp.sum(own_errors[:, None] * local_flat.astype(f32), axis=0)
    value_grad = lax.psum(value_part * factor, "dp")
    new_one = ((1.0 - polyak_rate) * t_one.astype(f32) + polyak_rate * q_one.astype(f32)).astype(
        bf16
    )
    new_two = ((1.0 - polyak_rate) * t_two.astype(f32) + polyak_rate * q_two.astype(f32)).astype(
        bf16
    )
    return (loss, head_one, head_two, value_grad, bias_grad.reshape(1), new_one, new_two)


def solution(mesh):
    in_specs = (
        P("dp", None, "mp"),
        P("dp", None),
        P("dp", None),
        P("dp"),
        P("dp", "mp"),
        P("dp", "mp"),
        P("dp", "mp"),
        P("dp", "mp"),
        P("dp", "mp"),
        P("mp"),
        P(),
    )
    out_specs = (P(), P("dp", "mp"), P("dp", "mp"), P("mp"), P(), P("dp", "mp"), P("dp", "mp"))
    return jax.shard_map(
        on_device, mesh=mesh, in_specs=in_specs, out_specs=out_specs, check_vma=False
    )
```

time: 1050 us -> 289 us (0.28)
  waiting for transfers between devices: 591 us -> 24.5 us
  blocking collectives: 315 us -> 200 us
  local copies, waits for them, and re-layouts: 35.7 us -> 7.53 us
  starting transfers between devices: 31.5 us -> 10.7 us
  matrix products: 31.2 us -> 10.8 us
  other arithmetic: 25.5 us -> 13.7 us
    all_gather x4 -> x2, waiting for transfers between devices: 333 us -> 24.5 us  [the longest x1 24.5 us: on_device(): all_back = lax.all_gather(back, 'dp', axis=0, tiled=True)]
    all_to_all x4 -> x2, waiting for transfers between devices: 255 us -> 0.01 us  [the longest x1 0.01 us: on_device(): spread = lax.all_to_all(flat, 'dp', split_axis=1, concat_axis=0, tiled=True)]
    psum x3 -> x2, blocking collectives: 306 us -> 55.9 us  [the longest x1 38.3 us: on_device(): all_scores = lax.psum(board, ('dp', 'mp'))]
    all_gather x1 -> x3, blocking collectives: 9.12 us -> 144 us  [the longest x1 103 us: on_device(): all_facts = lax.all_gather(facts, 'dp', axis=1, tiled=True)]
    mul x4 -> x1, local copies, waits for them, and re-layouts: 28.5 us -> 0.08 us  [on_device(): value_part = jnp.sum(own_errors[:, None] * local_flat.astype(f32), axis=0)]
    all_to_all x4 -> x2, starting transfers between devices: 31.4 us -> 10.6 us  [the longest x1 6.17 us: on_device(): spread = lax.all_to_all(flat, 'dp', split_axis=1, concat_axis=0, tiled=True)]
    dot_general x8, matrix products: 31.2 us -> 10.8 us  [the longest x1 3.11 us: on_device(): lax.dot_general(held, all_back[:, :cols], dims, preferred_element_type=f32)]
  transfers between devices with their start and end apart: 8 -> 4, of which waited for: 6 -> 1; matrix products, arithmetic and copies ran while one was open for 6% -> 5% of each run, Pallas kernels for 0% -> 0%
where the time goes in v1:
time: 289 us; the launch traced here: 286 us
  blocking collectives  200 us (69%)
  waiting for transfers between devices  24.5 us (8%)
  between operations  19.2 us (7%)
  other arithmetic  13.7 us (5%)
  matrix products  10.8 us (4%)
  starting transfers between devices  10.7 us (4%)
  local copies, waits for them, and re-layouts  7.53 us (3%)
    all_gather x1, blocking collectives, on_device(): all_facts = lax.all_gather(facts, 'dp', axis=1, tiled=True)  103 us
    psum x1, blocking collectives, on_device(): all_scores = lax.psum(board, ('dp', 'mp'))  38.3 us
    all_gather x1, blocking collectives, on_device(): all_ints = lax.all_gather(ints, 'dp', axis=0, tiled=True)  30.9 us
    all_gather x1, waiting for transfers between devices, on_device(): all_back = lax.all_gather(back, 'dp', axis=0, tiled=True)  24.5 us
    psum x1, blocking collectives, on_device(): value_grad = lax.psum(value_part * factor, 'dp')  17.6 us
    all_gather x1, blocking collectives, on_device(): wide = lax.all_gather(stacked, 'mp', axis=1, tiled=True)  9.62 us
    all_to_all x1, starting transfers between devices, on_device(): spread = lax.all_to_all(flat, 'dp', split_axis=1, concat_axis=0, tiled=True)  6.17 us
  transfers between devices with their start and end apart: 4, of which 1 were waited for; matrix products, arithmetic and copies ran while one was open for 5% of the time, Pallas kernels for 0%

profile of v1, /device:TPU:16, one launch (start us, length us, event | category | flops | bytes accessed | tf_op | source)
XLA Modules:
  0.0 286.4 jit_solution(14997182306145007077)
XLA Ops:
  7.2 0.7 reshape.239
  7.9 1.0 pad_maximum_fusion.1
  8.8 9.6 %all_gather.16 = bf16[129,3584]{1,0:T(8,128)(2,1)S(1)} all-gather(bf16[129,896]{1,0:T(8,128)(2,1)S(1)} %pad_maximum_fusion.1), channel_id=1, replica_groups=mesh['dp'=8,'mp'=4] {'mp'}, dimensions={1}, use_global_device_ids=true | all-gather | bytes 1155840 | tf_op jit(solution)/shard_map/all_gather | solution.py:42
  18.5 1.3 copy.34
  19.8 6.2 %all-to-all-start = ((bf16[128,8,448]{0,2,1:T(8,128)(2,1)}), bf16[128,8,448]{0,2,1:T(8,128)(2,1)S(1)}, u32[]{:S(2)}, u32[]{:S(2)}) async-start(bf16[128,8,448]{0,2,1:T(8,128)(2,1)} %bitcast.5), calls=%async_computation | async-start | bytes 1835008 | tf_op jit(solution)/shard_map/all_to_all | solution.py:92
  26.1 30.9 %all-gather.1 = s32[8,2,65]{2,1,0:T(2,128)S(1)} all-gather(s32[1,2,65]{2,1,0:T(2,128)S(1)} %add_bitcast_fusion), channel_id=1, replica_groups=mesh['dp'=8,'mp'=4] {'dp'}, dimensions={0}, use_global_device_ids=true | all-gather | bytes 4680 | tf_op jit(solution)/shard_map/all_gather | solution.py:54
  57.0 0.7 slice_reduce_fusion
  58.1 0.7 fusion.1
  58.8 0.7 convolution_convert_fusion
  59.6 0.4 copy-done.3
  60.0 0.7 convolution_convert_fusion.1
  60.7 0.4 copy-done.4
  61.1 0.7 convolution_convert_fusion.2
  61.8 0.4 copy-done.5
  62.2 0.7 convolution_convert_fusion.3
  63.0 2.0 pad_maximum_fusion
  65.0 4.5 %all-to-all-start.1 = ((bf16[8,64,3584]{2,1,0:T(8,128)(2,1)}), bf16[8,64,3584]{2,1,0:T(8,128)(2,1)}, u32[]{:S(2)}, u32[]{:S(2)}) async-start(bf16[8,64,3584]{2,1,0:T(8,128)(2,1)} %bitcast.50), calls=%async_computation.1 | async-start | bytes 7340032 | tf_op jit(solution)/shard_map/all_to_all | solution.py:103
  69.9 0.4 convert_reduce_fusion.1
  70.6 2.9 %gather_fusion = bf16[128,896]{1,0:T(8,128)(2,1)} fusion(bf16[19008,896]{1,0:T(8,128)(2,1)} %param.15, s32[1024]{0:T(1024)S(1)} %pad_clamp_fusion), kind=kCustom, calls=%fused_computation | custom fusion | bytes 459264 | tf_op jit(solution)/shard_map/gather | solution.py:86
  74.9 103.5 %all_gather.18 = f32[2,1024]{1,0:T(2,128)S(1)} all-gather(f32[2,128]{1,0:T(2,128)S(1)} %pad_maximum_fusion.4), channel_id=1, replica_groups=mesh['dp'=8,'mp'=4] {'dp'}, dimensions={1}, use_global_device_ids=true | all-gather | bytes 9216 | tf_op jit(solution)/shard_map/all_gather | solution.py:58
  178.6 0.7 select_reduce_fusion.1
  179.3 2.6 convert_reduce_fusion
  181.9 2.3 multiply_reduce_fusion.3
  184.4 38.3 %psum.14 = f32[4,512]{1,0:T(4,128)S(1)} all-reduce(f32[4,512]{1,0:T(4,128)S(1)} %dynamic_update_slice.3), channel_id=1, replica_groups=mesh['dp'=8,'mp'=4] {'dp','mp'}, use_global_device_ids=true, to_apply=%region_9.10 | all-reduce | flops 2048 | bytes 16384 | tf_op jit(solution)/shard_map/psum | solution.py:110
  222.7 0.6 fusion.46
  223.5 0.3 fusion.14
  223.8 0.7 pad_maximum_fusion.2
  225.4 3.2 %add_convert_fusion = (bf16[448,896]{1,0:T(8,128)(2,1)}, bf16[448,896]{1,0:T(8,128)(2,1)}) fusion(bf16[448,896]{1,0:T(8,128)(2,1)} %param.17, bf16[448,896]{1,0:T(8,128)(2,1)S(1)} %copy-done.2, bf16[448,896]{1,0:T(8,128)(2,1)} %param.16, bf16[448,896]{1,0:T(8,128)(2,1)S(1)} %copy-done.3), kind=kLoop, calls=%fused_computation.8 | loop fusion | flops 4816896 | bytes 4816896 | tf_op jit(solution)/shard_map/convert_element_type | solution.py:153
  230.3 17.6 %psum.15 = f32[896]{0:T(1024)} all-reduce(f32[896]{0:T(1024)S(1)} %broadcast_multiply_fusion), channel_id=1, replica_groups=mesh['dp'=8,'mp'=4] {'dp'}, use_global_device_ids=true, to_apply=%region_17.18 | all-reduce | flops 896 | bytes 7168 | tf_op jit(solution)/shard_map/psum | solution.py:149
  247.9 24.5 %all-gather.5.cloned.1.call-done = bf16[512,1792]{1,0:T(8,128)(2,1)} async-done(((bf16[64,1792]{1,0:T(8,128)(2,1)}), bf16[512,1792]{1,0:T(8,128)(2,1)}) %all-gather.5.cloned.1.call-update) | async-done | bytes 1835024 | tf_op jit(solution)/shard_map/all_gather | solution.py:135
  272.3 3.1 %convolution_multiply_fusion.1 = f32[448,896]{1,0:T(8,128)} fusion(bf16[512,448]{0,1:T(8,128)(2,1)S(1)} %fusion.1, bf16[512,1792]{1,0:T(8,128)(2,1)} %all-gather.5.cloned.1.call-done, f32[]{:T(128)S(6)} %div.30), kind=kOutput, calls=%fused_computation.11 | convolution fusion | flops 411443200 | bytes 2981892 | tf_op jit(solution)/shard_map/dot_general | solution.py:138
  275.5 1.8 convolution_multiply_fusion
  (68 shorter events, 3.1 us)
Async XLA Ops:
  18.5 7.5 %copy-start.8 = (s32[2]{0:T(128)S(1)}, s32[2]{0:T(128)}, u32[]{:S(2)}) copy-start(s32[2]{0:T(128)} %param.14) | copy-start | bytes 28
  18.5 7.6 %copy-start.6 = (s32[2,64]{1,0:T(2,128)S(1)}, s32[2,64]{1,0:T(2,128)}, u32[]{:S(2)}) copy-start(s32[2,64]{1,0:T(2,128)} %param.13) | copy-start | bytes 1540
  19.8 38.3 %all-to-all-start = ((bf16[128,8,448]{0,2,1:T(8,128)(2,1)}), bf16[128,8,448]{0,2,1:T(8,128)(2,1)S(1)}, u32[]{:S(2)}, u32[]{:S(2)}) async-start(bf16[128,8,448]{0,2,1:T(8,128)(2,1)} %bitcast.5), calls=%async_computation | async-start | bytes 1835008 | tf_op jit(solution)/shard_map/all_to_all | solution.py:92
  26.0 32.8 %copy-start.2 = (bf16[448,896]{1,0:T(8,128)(2,1)S(1)}, bf16[448,896]{1,0:T(8,128)(2,1)}, u32[]{:S(2)}) copy-start(bf16[448,896]{1,0:T(8,128)(2,1)} %param.19) | copy-start | bytes 2408452
  58.8 1.1 copy-start.3
  60.0 1.1 copy-start.4
  61.1 1.1 copy-start.5
  65.0 114.3 %all-to-all-start.1 = ((bf16[8,64,3584]{2,1,0:T(8,128)(2,1)}), bf16[8,64,3584]{2,1,0:T(8,128)(2,1)}, u32[]{:S(2)}, u32[]{:S(2)}) async-start(bf16[8,64,3584]{2,1,0:T(8,128)(2,1)} %bitcast.50), calls=%async_computation.1 | async-start | bytes 7340032 | tf_op jit(solution)/shard_map/all_to_all | solution.py:103
  69.4 5.3 %copy-start.7 = (f32[2,64]{1,0:T(2,128)S(1)}, f32[2,64]{1,0:T(2,128)}, u32[]{:S(2)}) copy-start(f32[2,64]{1,0:T(2,128)} %param.12) | copy-start | bytes 1540
  69.4 112.5 %all-gather.7.cloned.1.call-start = ((), (), s32[]{:S(2)}) async-start(), calls=%async_computation.3 | async-start | bytes 2064384 | tf_op jit(solution)/shard_map/all_gather | solution.py:87
  73.5 198.8 %all-gather.5.cloned.1.call-start = ((), (), s32[]{:S(2)}) async-start(), calls=%async_computation.2 | async-start | bytes 2064384 | tf_op jit(solution)/shard_map/all_gather | solution.py:135
  225.3 4.8 %copy-start.1 = (bf16[2,64,896]{2,1,0:T(8,128)(2,1)S(1)}, bf16[2,64,896]{2,1,0:T(8,128)(2,1)}, u32[]{:S(2)}) copy-start(bf16[2,64,896]{2,1,0:T(8,128)(2,1)} %param.11) | copy-start | bytes 688132
  272.3 3.1 %copy-start = (bf16[512,1792]{1,0:T(8,128)(2,1)S(1)}, bf16[512,1792]{1,0:T(8,128)(2,1)}, u32[]{:S(2)}) copy-start(bf16[512,1792]{1,0:T(8,128)(2,1)} %all-gather.5.cloned.1.call-done) | copy-start | bytes 5505028
Sparse Core Ops, SparseCore 0:
  73.7 82.6 all-gather.6
  224.7 47.6 all-gather.4

commit v2 on v1

--- a/solution.py
+++ b/solution.py
@@ -1,6 +1,10 @@
+import functools
+
 import jax
 import jax.numpy as jnp
 from jax import lax
+from jax.experimental import pallas as pl
+from jax.experimental.pallas import tpu as pltpu
 from jax.sharding import PartitionSpec as P
 
 discount = 0.99
@@ -17,6 +21,206 @@
 def slope(preact, upstream):
     _, pullback = jax.vjp(head_gelu, preact)
     return pullback(upstream)[0]
+
+
+MESH = pl.DeviceIdType.MESH
+
+
+def reduce_kernel(
+    dp, mp, held, seat, found, w_one, w_two, w_three, w_four, goal, worth,
+    back_out, score_out, value_out,
+    send_y, recv_y, sums, send_z, recv_z, pre, board, scores, backs, grads,
+    y_send, y_recv, z_send, z_recv, m_send, m_recv, s_send, s_recv, g_send, g_recv,
+    dz_send, dz_recv, dy_send, dy_recv,
+):
+    me = lax.axis_index("dp")
+    mine = lax.axis_index("mp")
+    half = dp // 2
+    z = lax.div(me, 2)
+    y = lax.rem(me, 2)
+    partner = z * 2 + (1 - y)
+    packed = held.shape[0]
+    share = packed // dp
+    side = half * share
+    cols = w_one.shape[1]
+    block = y * half + z
+    barrier = pltpu.get_barrier_semaphore()
+    for r in range(1, dp):
+        pl.semaphore_signal(
+            barrier, inc=1, device_id={"dp": lax.rem(me + r, dp)}, device_id_type=MESH
+        )
+    for r in range(1, mp):
+        pl.semaphore_signal(
+            barrier, inc=1, device_id={"mp": lax.rem(mine + r, mp)}, device_id_type=MESH
+        )
+    pl.semaphore_wait(barrier, dp + mp - 2)
+
+    def send(src, dst, one, two, axis, where):
+        copy = pltpu.make_async_remote_copy(
+            src_ref=src, dst_ref=dst, send_sem=one, recv_sem=two,
+            device_id={axis: where}, device_id_type=MESH,
+        )
+        copy.start()
+        return copy
+
+    theirs = pl.ds(pl.multiple_of((1 - y) * side, side), side)
+    ours = pl.ds(pl.multiple_of(y * side, side), side)
+    factors = ((seat, found), (held, w_one), (held, w_two), (held, w_three), (held, w_four))
+    tile = 128
+    y_copies = []
+    for k, (left, right) in enumerate(factors):
+
+        @pl.loop(0, cols // tile)
+        def _(c):
+            at = pl.ds(pl.multiple_of(c * tile, tile), tile)
+            send_y[k, :, at] = jnp.dot(
+                left[theirs, :], right[:, at], preferred_element_type=f32
+            ).astype(bf16)
+
+        y_copies.append(
+            send(send_y.at[k], recv_y.at[k], y_send.at[k], y_recv.at[k], "dp", partner)
+        )
+
+        @pl.loop(0, cols // tile)
+        def _(c):
+            at = pl.ds(pl.multiple_of(c * tile, tile), tile)
+            sums[k, :, at] = jnp.dot(left[ours, :], right[:, at], preferred_element_type=f32)
+
+    z_copies = []
+    for k in range(5):
+        y_copies[k].wait()
+
+        @pl.loop(0, half)
+        def _(h):
+            at = pl.ds(pl.multiple_of(h * share, share), share)
+            total = sums[k, at, :] + recv_y[k, at, :].astype(f32)
+            sums[k, at, :] = total
+            send_z[k, h] = total.astype(bf16)
+
+        for r in range(1, half):
+            to = lax.rem(z + r, half)
+            z_copies.append(
+                send(
+                    send_z.at[k, to], recv_z.at[k, r - 1], z_send.at[k, r - 1],
+                    z_recv.at[k, r - 1], "dp", to * 2 + y,
+                )
+            )
+    lane = lax.broadcasted_iota(jnp.int32, (share, 128), 1)
+    mine_at = pl.ds(pl.multiple_of(z * share, share), share)
+    marks = jnp.zeros((share, 128), f32)
+    for k in range(5):
+        total = sums[k, mine_at, :]
+        for r in range(1, half):
+            z_copies[k * (half - 1) + r - 1].wait()
+            total = total + recv_z[k, r - 1].astype(f32)
+        pre[k] = total
+        if k > 0:
+            score = jnp.sum(head_gelu(total) * pre[0], axis=1, keepdims=True)
+            marks = jnp.where(lane == k - 1, score, marks)
+    board[mine] = marks
+    m_copies = [
+        send(
+            board.at[mine], board.at[mine], m_send.at[r - 1], m_recv.at[r - 1], "mp",
+            lax.rem(mine + r, mp),
+        )
+        for r in range(1, mp)
+    ]
+    for copy in m_copies:
+        copy.wait()
+    full = board[0]
+    for r in range(1, mp):
+        full = full + board[r]
+    scores[block] = full
+    s_copies = [
+        send(
+            scores.at[block], scores.at[block], s_send.at[r - 1], s_recv.at[r - 1], "dp",
+            lax.rem(me + r, dp),
+        )
+        for r in range(1, dp)
+    ]
+    own_goal = goal[pl.ds(pl.multiple_of(block * share, share), share), :]
+    for k in range(2):
+        up = 2.0 * (full[:, k : k + 1] - own_goal)
+        backs[block, :, k * cols : (k + 1) * cols] = slope(pre[k + 1], up * pre[0]).astype(bf16)
+    dz_copies = [
+        send(
+            backs.at[block], backs.at[block], dz_send.at[r - 1], dz_recv.at[r - 1], "dp",
+            lax.rem(z + r, half) * 2 + y,
+        )
+        for r in range(1, half)
+    ]
+    dy_copies = [
+        send(backs.at[block], backs.at[block], dy_send.at[0], dy_recv.at[0], "dp", partner)
+    ]
+    for copy in s_copies:
+        copy.wait()
+    grad = jnp.zeros((1, held.shape[1]), f32)
+    for h in range(dp):
+        at = slice(h * share, (h + 1) * share)
+        gap = jnp.minimum(scores[h, :, 2:3], scores[h, :, 3:4]) - worth[at, :]
+        weight = jnp.where(gap < 0.0, 1.0 - expectile, expectile)
+        error = -2.0 * weight * gap
+        grad = grad + jnp.sum(error * held[at, :].astype(f32), axis=0, keepdims=True)
+    grads[me] = jnp.broadcast_to(grad, (8, held.shape[1]))
+    g_copies = [
+        send(
+            grads.at[me], grads.at[me], g_send.at[r - 1], g_recv.at[r - 1], "dp",
+            lax.rem(me + r, dp),
+        )
+        for r in range(1, dp)
+    ]
+    for r in range(1, half):
+        dz_copies[r - 1].wait()
+        seen = y * half + lax.rem(z + half - r, half)
+        dy_copies.append(
+            send(backs.at[seen], backs.at[seen], dy_send.at[r], dy_recv.at[r], "dp", partner)
+        )
+    for copy in g_copies:
+        copy.wait()
+    value_out[...] = grads[...]
+    score_out[...] = scores[...]
+    for copy in dy_copies:
+        copy.wait()
+    back_out[...] = backs[...]
+
+
+def reduce_call(dp, mp, held, seat, found, weights, goal, worth):
+    packed, rows = held.shape
+    cols = weights[0].shape[1]
+    half = dp // 2
+    share = packed // dp
+    side = share * half
+    dma = pltpu.SemaphoreType.DMA
+    vmem = pl.BlockSpec(memory_space=pltpu.VMEM)
+    return pl.pallas_call(
+        functools.partial(reduce_kernel, dp, mp),
+        out_shape=(
+            jax.ShapeDtypeStruct((dp, share, 2 * cols), bf16),
+            jax.ShapeDtypeStruct((dp, share, 128), f32),
+            jax.ShapeDtypeStruct((dp, 8, rows), f32),
+        ),
+        in_specs=[vmem] * 9,
+        out_specs=(vmem, vmem, vmem),
+        scratch_shapes=[
+            pltpu.VMEM((5, side, cols), bf16),
+            pltpu.VMEM((5, side, cols), bf16),
+            pltpu.VMEM((5, side, cols), f32),
+            pltpu.VMEM((5, half, share, cols), bf16),
+            pltpu.VMEM((5, half - 1, share, cols), bf16),
+            pltpu.VMEM((5, share, cols), f32),
+            pltpu.VMEM((mp, share, 128), f32),
+            pltpu.VMEM((dp, share, 128), f32),
+            pltpu.VMEM((dp, share, 2 * cols), bf16),
+            pltpu.VMEM((dp, 8, rows), f32),
+            dma((5,)), dma((5,)), dma((5, half - 1)), dma((5, half - 1)),
+            dma((mp - 1,)), dma((mp - 1,)), dma((dp - 1,)), dma((dp - 1,)),
+            dma((dp - 1,)), dma((dp - 1,)), dma((half - 1,)), dma((half - 1,)),
+            dma((half,)), dma((half,)),
+        ],
+        compiler_params=pltpu.CompilerParams(
+            collective_id=1, has_side_effects=True, vmem_limit_bytes=56 << 20
+        ),
+    )(held, seat, found, *weights, goal, worth)
 
 
 def pick(mask, row):
@@ -84,34 +288,44 @@
     wanted = jnp.arange(own, dtype=jnp.int32)[:, None] + me * own == where_held[None, :]
     requests = pick(wanted, ids - me * local_rows)
     found = table[requests]
-    all_found = lax.all_gather(found, "dp", axis=0, tiled=True)
-    seat = pick(own_mask, where_held)
-    seat_mask = (jnp.arange(total, dtype=jnp.int32)[None, :] == seat[:, None]).astype(bf16)
-    embed = jnp.dot(seat_mask, all_found, preferred_element_type=f32)
 
     spread = lax.all_to_all(flat, "dp", split_axis=1, concat_axis=0, tiled=True)
     pack_mask = (jnp.arange(packed, dtype=jnp.int32)[:, None] == place[None, :]).astype(bf16)
     held = jnp.dot(pack_mask, spread, preferred_element_type=f32).astype(bf16)
 
-    partial = jnp.concatenate(
-        [
-            jnp.dot(held, weight, preferred_element_type=f32).astype(bf16)
-            for weight in (q_one, q_two, t_one, t_two)
-        ],
-        axis=1,
-    )
-    swapped = lax.all_to_all(partial, "dp", split_axis=0, concat_axis=0, tiled=True)
-    pre = jnp.sum(swapped.reshape(dp, share, 4 * cols).astype(f32), axis=0)
-    pres = [pre[:, k * cols : (k + 1) * cols] for k in range(4)]
-    scores = jnp.stack([jnp.sum(head_gelu(p) * embed, axis=1) for p in pres])
-    board = lax.dynamic_update_slice(
-        jnp.zeros((4, packed), f32), scores, (jnp.zeros((), jnp.int32), me * share)
-    )
-    all_scores = lax.psum(board, ("dp", "mp"))
-
     pack_bool = jnp.arange(packed, dtype=jnp.int32)[:, None] == place[None, :]
     goal = pick(pack_bool, all_facts[0])
     worth = pick(pack_bool, all_facts[1])
+    in_vmem = 30 * packed * cols < (32 << 20)
+    if in_vmem:
+        seats = pick(pack_bool, where_held) - me * own
+        seat = (seats[:, None] == jnp.arange(own, dtype=jnp.int32)[None, :]).astype(bf16)
+        backs, tiles, grads = reduce_call(
+            dp, lax.axis_size("mp"), held, seat, found, (q_one, q_two, t_one, t_two),
+            goal[:, None], worth[:, None],
+        )
+        all_scores = tiles.reshape(packed, 128)[:, :4].T
+    else:
+        all_found = lax.all_gather(found, "dp", axis=0, tiled=True)
+        seat = pick(own_mask, where_held)
+        seat_mask = (jnp.arange(total, dtype=jnp.int32)[None, :] == seat[:, None]).astype(bf16)
+        embed = jnp.dot(seat_mask, all_found, preferred_element_type=f32)
+        partial = jnp.concatenate(
+            [
+                jnp.dot(held, weight, preferred_element_type=f32).astype(bf16)
+                for weight in (q_one, q_two, t_one, t_two)
+            ],
+            axis=1,
+        )
+        swapped = lax.all_to_all(partial, "dp", split_axis=0, concat_axis=0, tiled=True)
+        pre = jnp.sum(swapped.reshape(dp, share, 4 * cols).astype(f32), axis=0)
+        pres = [pre[:, k * cols : (k + 1) * cols] for k in range(4)]
+        scores = jnp.stack([jnp.sum(head_gelu(p) * embed, axis=1) for p in pres])
+        board = lax.dynamic_update_slice(
+            jnp.zeros((4, packed), f32), scores, (jnp.zeros((), jnp.int32), me * share)
+        )
+        all_scores = lax.psum(board, ("dp", "mp"))
+
     lowest = jnp.minimum(all_scores[2], all_scores[3])
     spread_to = lowest - worth
     weights = jnp.where(spread_to < 0.0, 1.0 - expectile, expectile)
@@ -123,16 +337,19 @@
     grad_values = -2.0 * weights * spread_to
     bias_grad = jnp.sum(grad_values) * factor
 
-    up_one = lax.dynamic_slice(2.0 * err_one, (me * share,), (share,))
-    up_two = lax.dynamic_slice(2.0 * err_two, (me * share,), (share,))
-    back = jnp.concatenate(
-        [
-            slope(pres[0], up_one[:, None] * embed).astype(bf16),
-            slope(pres[1], up_two[:, None] * embed).astype(bf16),
-        ],
-        axis=1,
-    )
-    all_back = lax.all_gather(back, "dp", axis=0, tiled=True)
+    if in_vmem:
+        all_back = backs.reshape(packed, 2 * cols)
+    else:
+        up_one = lax.dynamic_slice(2.0 * err_one, (me * share,), (share,))
+        up_two = lax.dynamic_slice(2.0 * err_two, (me * share,), (share,))
+        back = jnp.concatenate(
+            [
+                slope(pres[0], up_one[:, None] * embed).astype(bf16),
+                slope(pres[1], up_two[:, None] * embed).astype(bf16),
+            ],
+            axis=1,
+        )
+        all_back = lax.all_gather(back, "dp", axis=0, tiled=True)
     dims = (((0,), (0,)), ((), ()))
     head_one = (
         lax.dot_general(held, all_back[:, :cols], dims, preferred_element_type=f32) * factor
@@ -141,12 +358,18 @@
         lax.dot_general(held, all_back[:, cols:], dims, preferred_element_type=f32) * factor
     )
 
-    own_place = lax.dynamic_slice(place, (me * own,), (own,))
-    own_errors = pick(
-        own_place[:, None] == jnp.arange(packed, dtype=jnp.int32)[None, :], grad_values
-    )
-    value_part = jnp.sum(own_errors[:, None] * local_flat.astype(f32), axis=0)
-    value_grad = lax.psum(value_part * factor, "dp")
+    if in_vmem:
+        features = grads[:, 0, :].reshape(dp * rows)
+        value_grad = (
+            lax.dynamic_slice(features, (lax.axis_index("mp") * width,), (width,)) * factor
+        )
+    else:
+        own_place = lax.dynamic_slice(place, (me * own,), (own,))
+        own_errors = pick(
+            own_place[:, None] == jnp.arange(packed, dtype=jnp.int32)[None, :], grad_values
+        )
+        value_part = jnp.sum(own_errors[:, None] * local_flat.astype(f32), axis=0)
+        value_grad = lax.psum(value_part * factor, "dp")
     new_one = ((1.0 - polyak_rate) * t_one.astype(f32) + polyak_rate * q_one.astype(f32)).astype(
         bf16
     )

time: 289 us -> 207 us (0.72)
  blocking collectives: 200 us -> 53.9 us
  Pallas kernels: 0 us -> 115 us
  waiting for transfers between devices: 24.5 us -> 0.01 us
  between operations: 19.2 us -> 5.71 us
  other arithmetic: 13.7 us -> 7.87 us
  starting transfers between devices: 10.7 us -> 6.3 us
  matrix products: 10.8 us -> 7.65 us
    pallas_call x0 -> x1, Pallas kernels: none -> 115 us  [reduce_call(): pl.pallas_call(functools.partial(reduce_kernel, dp, mp), out_shape=(jax.S...]
    all_gather x1, blocking collectives: 103 us -> 13.4 us  [on_device(): all_facts = lax.all_gather(facts, 'dp', axis=1, tiled=True)]
    psum x2 -> x0, blocking collectives: 55.9 us -> none  [the longest x1 38.3 us: on_device(): all_scores = lax.psum(board, ('dp', 'mp'))]
    all_gather x2 -> x0, waiting for transfers between devices: 24.5 us -> none  [the longest x1 24.5 us: on_device(): all_back = lax.all_gather(back, 'dp', axis=0, tiled=True)]
    dot_general x5 -> x0, matrix products: 5.19 us -> none  [the longest x4 2.91 us: on_device(): jnp.dot(held, weight, preferred_element_type=f32).astype(bf16)]
    all_to_all x1 -> x0, starting transfers between devices: 4.45 us -> none  [on_device(): lax.all_to_all(partial, 'dp', split_axis=0, concat_axis=0, tiled=True)]
  transfers between devices with their start and end apart: 4 -> 1, of which waited for: 1 -> 0; matrix products, arithmetic and copies ran while one was open for 5% -> 5% of each run, Pallas kernels for 0% -> 0%
where the time goes in v2:
time: 207 us; the launch traced here: 206 us
  Pallas kernels  115 us (56%)
  blocking collectives  53.9 us (26%)
  local copies, waits for them, and re-layouts  8.71 us (4%)
  other arithmetic  7.87 us (4%)
  matrix products  7.65 us (4%)
  starting transfers between devices  6.3 us (3%)
  between operations  5.71 us (3%)
    pallas_call x1, Pallas kernels, reduce_call(): pl.pallas_call(functools.partial(reduce_kernel, dp, mp), out_shape=(jax.S...  115 us
    all_gather x1, blocking collectives, on_device(): all_ints = lax.all_gather(ints, 'dp', axis=0, tiled=True)  30.9 us
    all_gather x1, blocking collectives, on_device(): all_facts = lax.all_gather(facts, 'dp', axis=1, tiled=True)  13.4 us
    all_gather x1, blocking collectives, on_device(): wide = lax.all_gather(stacked, 'mp', axis=1, tiled=True)  9.62 us
    all_to_all x1, starting transfers between devices, on_device(): spread = lax.all_to_all(flat, 'dp', split_axis=1, concat_axis=0, tiled=True)  6.3 us
  transfers between devices with their start and end apart: 1, of which 0 were waited for; matrix products, arithmetic and copies ran while one was open for 5% of the time, Pallas kernels for 0%

profile of v2, /device:TPU:16, one launch (start us, length us, event | category | flops | bytes accessed | tf_op | source)
XLA Modules:
  0.0 205.6 jit_solution(10112953717663066033)
XLA Ops:
  0.6 0.7 reshape.223
  1.3 1.0 pad_maximum_fusion
  2.3 9.6 %all_gather.10 = bf16[129,3584]{1,0:T(8,128)(2,1)S(1)} all-gather(bf16[129,896]{1,0:T(8,128)(2,1)S(1)} %pad_maximum_fusion), channel_id=1, replica_groups=mesh['dp'=8,'mp'=4] {'mp'}, dimensions={1}, use_global_device_ids=true | all-gather | bytes 1155840 | tf_op jit(solution)/shard_map/all_gather | solution.py:246
  12.0 1.3 copy.47
  13.3 6.3 %all-to-all-start = ((bf16[128,8,448]{0,2,1:T(8,128)(2,1)}), bf16[128,8,448]{0,2,1:T(8,128)(2,1)}, u32[]{:S(2)}, u32[]{:S(2)}) async-start(bf16[128,8,448]{0,2,1:T(8,128)(2,1)} %bitcast.5), calls=%async_computation | async-start | bytes 1835008 | tf_op jit(solution)/shard_map/all_to_all | solution.py:292
  19.6 0.1 copy.45
  19.8 30.9 %all-gather = s32[8,2,65]{2,1,0:T(2,128)S(1)} all-gather(s32[1,2,65]{2,1,0:T(2,128)S(1)} %add_bitcast_fusion), channel_id=1, replica_groups=mesh['dp'=8,'mp'=4] {'dp'}, dimensions={0}, use_global_device_ids=true | all-gather | bytes 4680 | tf_op jit(solution)/shard_map/all_gather | solution.py:258
  50.7 0.1 and.34
  50.7 0.1 and.33
  50.8 0.7 slice_reduce_fusion.1
  53.1 0.1 select_reduce_fusion.4
  53.5 0.3 multiply_reduce_fusion
  53.8 0.1 add.140
  54.0 0.1 stack_reshape.4
  54.1 13.4 %all_gather.11 = f32[2,1024]{1,0:T(2,128)S(1)} all-gather(f32[2,128]{1,0:T(2,128)S(1)} %pad_maximum_fusion.1), channel_id=1, replica_groups=mesh['dp'=8,'mp'=4] {'dp'}, dimensions={1}, use_global_device_ids=true | all-gather | bytes 9216 | tf_op jit(solution)/shard_map/all_gather | solution.py:262
  67.5 0.7 select_reduce_fusion
  68.2 0.9 copy.50.goal
  69.0 0.9 copy.51.worth
  70.0 0.4 convert_reduce_fusion
  70.4 0.2 select_reduce_fusion.3
  70.6 2.9 %gather_fusion = bf16[128,896]{1,0:T(8,128)(2,1)} fusion(bf16[19008,896]{1,0:T(8,128)(2,1)} %param.15, s32[1024]{0:T(1024)S(1)} %pad_clamp_fusion), kind=kCustom, calls=%fused_computation | custom fusion | bytes 459264 | tf_op jit(solution)/shard_map/gather | solution.py:290
  73.6 0.3 select_reduce_fusion.2
  73.8 0.8 fusion.7.seat
  74.6 1.8 add_convert_fusion
  76.4 2.7 %fusion.1.held = bf16[512,448]{1,0:T(8,128)(2,1)} fusion(s32[1024]{0:T(1024)S(1)} %select_n.72, bf16[128,8,448]{0,2,1:T(8,128)(2,1)} %all-to-all-done), kind=kOutput, calls=%fused_computation.11 | convolution fusion | flops 470515712 | bytes 1380352 | tf_op jit(solution)/shard_map/dot_general | solution.py:294
  79.1 115.4 %shard_map.162 = (bf16[8,64,1792]{2,1,0:T(8,128)(2,1)}, f32[8,64,128]{2,1,0:T(8,128)}, f32[8,8,448]{2,1,0:T(8,128)}) custom-call(bf16[512,448]{1,0:T(8,128)(2,1)} %fusion.1.held, bf16[512,128]{1,0:T(8,128)(2,1)} %fusion.7.seat, bf16[128,896]{1,0:T(8,128)(2,1)} %gather_fusion, bf16[448,896]{1,0:T(8,128)(2,1)} %w_one.1, bf16[448,896]{1,0:T(8,128)(2,1)} %w_two.1, ...), custom_call_target="tpu_custom_call" | custom-call | tf_op jit(solution)/shard_map/pallas_call | solution.py:195
  194.6 3.1 %convolution_multiply_fusion = f32[448,896]{1,0:T(8,128)} fusion(bf16[512,448]{1,0:T(8,128)(2,1)S(1)} %copy-done, bf16[512,1792]{1,0:T(8,128)(2,1)} %bitcast.40, f32[]{:T(128)S(6)} %div.30), kind=kOutput, calls=%fused_computation.9 | convolution fusion | flops 411443200 | bytes 2981892 | tf_op jit(solution)/shard_map/dot_general | solution.py:358
  197.7 1.8 convolution_multiply_fusion.1
  199.6 0.1 copy.55
  199.7 0.6 fusion.13
  201.6 0.9 slice_reduce_fusion
  202.6 0.7 dynamic-slice_multiply_fusion
  (49 shorter events, 1.1 us)
Async XLA Ops:
  12.0 7.6 %copy-start.9 = (s32[2]{0:T(128)S(1)}, s32[2]{0:T(128)}, u32[]{:S(2)}) copy-start(s32[2]{0:T(128)} %param.14) | copy-start | bytes 28
  12.0 7.7 %copy-start.7 = (s32[2,64]{1,0:T(2,128)S(1)}, s32[2,64]{1,0:T(2,128)}, u32[]{:S(2)}) copy-start(s32[2,64]{1,0:T(2,128)} %param.13) | copy-start | bytes 1540
  13.3 40.7 %copy-start.8 = (f32[2,64]{1,0:T(2,128)S(1)}, f32[2,64]{1,0:T(2,128)}, u32[]{:S(2)}) copy-start(f32[2,64]{1,0:T(2,128)} %param.12) | copy-start | bytes 1540
  13.3 63.2 %all-to-all-start = ((bf16[128,8,448]{0,2,1:T(8,128)(2,1)}), bf16[128,8,448]{0,2,1:T(8,128)(2,1)}, u32[]{:S(2)}, u32[]{:S(2)}) async-start(bf16[128,8,448]{0,2,1:T(8,128)(2,1)} %bitcast.5), calls=%async_computation | async-start | bytes 1835008 | tf_op jit(solution)/shard_map/all_to_all | solution.py:292
  53.5 21.2 %copy-start.1 = (bf16[448,896]{1,0:T(8,128)(2,1)S(1)}, bf16[448,896]{1,0:T(8,128)(2,1)}, u32[]{:S(2)}) copy-start(bf16[448,896]{1,0:T(8,128)(2,1)} %w_one.1) | copy-start | bytes 2408452
  53.5 21.2 %copy-start.2 = (bf16[448,896]{1,0:T(8,128)(2,1)S(1)}, bf16[448,896]{1,0:T(8,128)(2,1)}, u32[]{:S(2)}) copy-start(bf16[448,896]{1,0:T(8,128)(2,1)} %w_two.1) | copy-start | bytes 2408452
  53.5 21.2 %copy-start.3 = (bf16[448,896]{1,0:T(8,128)(2,1)S(1)}, bf16[448,896]{1,0:T(8,128)(2,1)}, u32[]{:S(2)}) copy-start(bf16[448,896]{1,0:T(8,128)(2,1)} %w_three.1) | copy-start | bytes 2408452
  53.8 20.9 %copy-start.4 = (bf16[448,896]{1,0:T(8,128)(2,1)S(1)}, bf16[448,896]{1,0:T(8,128)(2,1)}, u32[]{:S(2)}) copy-start(bf16[448,896]{1,0:T(8,128)(2,1)} %w_four.1) | copy-start | bytes 2408452
  79.1 115.5 %copy-start = (bf16[512,448]{1,0:T(8,128)(2,1)S(1)}, bf16[512,448]{1,0:T(8,128)(2,1)}, u32[]{:S(2)}) copy-start(bf16[512,448]{1,0:T(8,128)(2,1)} %fusion.1.held) | copy-start | bytes 1376260
  194.6 3.2 %copy-start.5 = (bf16[8,64,1792]{2,1,0:T(8,128)(2,1)S(1)}, bf16[8,64,1792]{2,1,0:T(8,128)(2,1)}, u32[]{:S(2)}) copy-start(bf16[8,64,1792]{2,1,0:T(8,128)(2,1)} %get-tuple-element.11) | copy-start | bytes 5505028
  197.7 1.8 copy-start.6

commit v3 on v2

--- a/solution.py
+++ b/solution.py
@@ -86,8 +86,9 @@
             at = pl.ds(pl.multiple_of(c * tile, tile), tile)
             sums[k, :, at] = jnp.dot(left[ours, :], right[:, at], preferred_element_type=f32)
 
-    z_copies = []
-    for k in range(5):
+    z_copies = {}
+
+    def along_z(k):
         y_copies[k].wait()
 
         @pl.loop(0, half)
@@ -97,39 +98,67 @@
             sums[k, at, :] = total
             send_z[k, h] = total.astype(bf16)
 
+        z_copies[k] = []
         for r in range(1, half):
             to = lax.rem(z + r, half)
-            z_copies.append(
+            z_copies[k].append(
                 send(
                     send_z.at[k, to], recv_z.at[k, r - 1], z_send.at[k, r - 1],
                     z_recv.at[k, r - 1], "dp", to * 2 + y,
                 )
             )
+
     lane = lax.broadcasted_iota(jnp.int32, (share, 128), 1)
     mine_at = pl.ds(pl.multiple_of(z * share, share), share)
-    marks = jnp.zeros((share, 128), f32)
-    for k in range(5):
+
+    def finish(k):
         total = sums[k, mine_at, :]
         for r in range(1, half):
-            z_copies[k * (half - 1) + r - 1].wait()
+            z_copies[k][r - 1].wait()
             total = total + recv_z[k, r - 1].astype(f32)
         pre[k] = total
-        if k > 0:
-            score = jnp.sum(head_gelu(total) * pre[0], axis=1, keepdims=True)
+
+    def over_mp(pair, first):
+        marks = jnp.zeros((share, 128), f32)
+        for k in (first, first + 1):
+            finish(k)
+            score = jnp.sum(head_gelu(pre[k]) * pre[0], axis=1, keepdims=True)
             marks = jnp.where(lane == k - 1, score, marks)
-    board[mine] = marks
-    m_copies = [
+        board[pair, mine] = marks
+        m_copies = [
+            send(
+                board.at[pair, mine], board.at[pair, mine], m_send.at[pair, r - 1],
+                m_recv.at[pair, r - 1], "mp", lax.rem(mine + r, mp),
+            )
+            for r in range(1, mp)
+        ]
+        for copy in m_copies:
+            copy.wait()
+        full = board[pair, 0]
+        for r in range(1, mp):
+            full = full + board[pair, r]
+        return full
+
+    for k in range(4):
+        along_z(k)
+    finish(0)
+    full = over_mp(0, 1)
+    own_goal = goal[pl.ds(pl.multiple_of(block * share, share), share), :]
+    for k in range(2):
+        up = 2.0 * (full[:, k : k + 1] - own_goal)
+        backs[block, :, k * cols : (k + 1) * cols] = slope(pre[k + 1], up * pre[0]).astype(bf16)
+    along_z(4)
+    dz_copies = [
         send(
-            board.at[mine], board.at[mine], m_send.at[r - 1], m_recv.at[r - 1], "mp",
-            lax.rem(mine + r, mp),
-        )
-        for r in range(1, mp)
-    ]
-    for copy in m_copies:
-        copy.wait()
-    full = board[0]
-    for r in range(1, mp):
-        full = full + board[r]
+            backs.at[block], backs.at[block], dz_send.at[r - 1], dz_recv.at[r - 1], "dp",
+            lax.rem(z + r, half) * 2 + y,
+        )
+        for r in range(1, half)
+    ]
+    dy_copies = [
+        send(backs.at[block], backs.at[block], dy_send.at[0], dy_recv.at[0], "dp", partner)
+    ]
+    full = full + over_mp(1, 3)
     scores[block] = full
     s_copies = [
         send(
@@ -138,20 +167,12 @@
         )
         for r in range(1, dp)
     ]
-    own_goal = goal[pl.ds(pl.multiple_of(block * share, share), share), :]
-    for k in range(2):
-        up = 2.0 * (full[:, k : k + 1] - own_goal)
-        backs[block, :, k * cols : (k + 1) * cols] = slope(pre[k + 1], up * pre[0]).astype(bf16)
-    dz_copies = [
-        send(
-            backs.at[block], backs.at[block], dz_send.at[r - 1], dz_recv.at[r - 1], "dp",
-            lax.rem(z + r, half) * 2 + y,
-        )
-        for r in range(1, half)
-    ]
-    dy_copies = [
-        send(backs.at[block], backs.at[block], dy_send.at[0], dy_recv.at[0], "dp", partner)
-    ]
+    for r in range(1, half):
+        dz_copies[r - 1].wait()
+        seen = y * half + lax.rem(z + half - r, half)
+        dy_copies.append(
+            send(backs.at[seen], backs.at[seen], dy_send.at[r], dy_recv.at[r], "dp", partner)
+        )
     for copy in s_copies:
         copy.wait()
     grad = jnp.zeros((1, held.shape[1]), f32)
@@ -169,12 +190,6 @@
         )
         for r in range(1, dp)
     ]
-    for r in range(1, half):
-        dz_copies[r - 1].wait()
-        seen = y * half + lax.rem(z + half - r, half)
-        dy_copies.append(
-            send(backs.at[seen], backs.at[seen], dy_send.at[r], dy_recv.at[r], "dp", partner)
-        )
     for copy in g_copies:
         copy.wait()
     value_out[...] = grads[...]
@@ -208,12 +223,12 @@
             pltpu.VMEM((5, half, share, cols), bf16),
             pltpu.VMEM((5, half - 1, share, cols), bf16),
             pltpu.VMEM((5, share, cols), f32),
-            pltpu.VMEM((mp, share, 128), f32),
+            pltpu.VMEM((2, mp, share, 128), f32),
             pltpu.VMEM((dp, share, 128), f32),
             pltpu.VMEM((dp, share, 2 * cols), bf16),
             pltpu.VMEM((dp, 8, rows), f32),
             dma((5,)), dma((5,)), dma((5, half - 1)), dma((5, half - 1)),
-            dma((mp - 1,)), dma((mp - 1,)), dma((dp - 1,)), dma((dp - 1,)),
+            dma((2, mp - 1)), dma((2, mp - 1)), dma((dp - 1,)), dma((dp - 1,)),
             dma((dp - 1,)), dma((dp - 1,)), dma((half - 1,)), dma((half - 1,)),
             dma((half,)), dma((half,)),
         ],
@@ -221,6 +236,114 @@
             collective_id=1, has_side_effects=True, vmem_limit_bytes=56 << 20
         ),
     )(held, seat, found, *weights, goal, worth)
+
+
+def spread_kernel(
+    dp, mp, hid, ints, rewards, parts,
+    hid_out, int_out, float_out,
+    wide, landed, marks, sums, facts,
+    a_send, a_recv, b_send, b_recv, i_send, i_recv, v_send, v_recv, f_send, f_recv,
+):
+    me = lax.axis_index("dp")
+    mine = lax.axis_index("mp")
+    per = dp // mp
+    barrier = pltpu.get_barrier_semaphore()
+    for r in range(1, dp):
+        pl.semaphore_signal(
+            barrier, inc=1, device_id={"dp": lax.rem(me + r, dp)}, device_id_type=MESH
+        )
+    for r in range(1, mp):
+        pl.semaphore_signal(
+            barrier, inc=1, device_id={"mp": lax.rem(mine + r, mp)}, device_id_type=MESH
+        )
+    pl.semaphore_wait(barrier, dp + mp - 2)
+
+    def send(src, dst, one, two, axis, where):
+        copy = pltpu.make_async_remote_copy(
+            src_ref=src, dst_ref=dst, send_sem=one, recv_sem=two,
+            device_id={axis: where}, device_id_type=MESH,
+        )
+        copy.start()
+        return copy
+
+    blocks = pl.ds(mine * per, per)
+    v_copies = [
+        send(
+            parts, sums.at[mine], v_send.at[r - 1], v_recv.at[r - 1], "mp", lax.rem(mine + r, mp)
+        )
+        for r in range(1, mp)
+    ]
+    a_copies = [
+        send(
+            hid, wide.at[blocks], a_send.at[r - 1], a_recv.at[r - 1], "mp", lax.rem(mine + r, mp)
+        )
+        for r in range(1, mp)
+    ]
+    i_copies = [
+        send(ints, marks.at[me], i_send.at[r - 1], i_recv.at[r - 1], "dp", lax.rem(me + r, dp))
+        for r in range(1, dp)
+    ]
+    wide[blocks] = hid[...]
+    sums[mine] = parts[...]
+    marks[me] = ints[...]
+    for copy in v_copies:
+        copy.wait()
+    total = sums[0]
+    for r in range(1, mp):
+        total = total + sums[r]
+    row = lax.broadcasted_iota(jnp.int32, total.shape, 0)
+    facts[me] = jnp.where(row == 0, rewards[...], total)
+    for copy in a_copies:
+        copy.wait()
+    b_copies = []
+    for r in range(1, dp):
+        to = lax.rem(me + r, dp)
+        b_copies.append(
+            send(wide.at[to], landed.at[me], b_send.at[r - 1], b_recv.at[r - 1], "dp", to)
+        )
+    f_copies = [
+        send(facts.at[me], facts.at[me], f_send.at[r - 1], f_recv.at[r - 1], "dp", lax.rem(me + r, dp))
+        for r in range(1, dp)
+    ]
+    landed[me] = wide[me]
+    for copy in i_copies:
+        copy.wait()
+    int_out[...] = marks[...]
+    for copy in f_copies:
+        copy.wait()
+    float_out[...] = facts[...]
+    for copy in b_copies:
+        copy.wait()
+    hid_out[...] = landed[...]
+
+
+def spread_call(dp, mp, hid, ints, rewards, parts):
+    dma = pltpu.SemaphoreType.DMA
+    vmem = pl.BlockSpec(memory_space=pltpu.VMEM)
+    shape = (dp,) + hid.shape[1:]
+    return pl.pallas_call(
+        functools.partial(spread_kernel, dp, mp),
+        out_shape=(
+            jax.ShapeDtypeStruct(shape, bf16),
+            jax.ShapeDtypeStruct((dp,) + ints.shape, jnp.int32),
+            jax.ShapeDtypeStruct((dp,) + parts.shape, f32),
+        ),
+        in_specs=[vmem] * 4,
+        out_specs=(vmem, vmem, vmem),
+        scratch_shapes=[
+            pltpu.VMEM(shape, bf16),
+            pltpu.VMEM(shape, bf16),
+            pltpu.VMEM((dp,) + ints.shape, jnp.int32),
+            pltpu.VMEM((mp,) + parts.shape, f32),
+            pltpu.VMEM((dp,) + parts.shape, f32),
+            dma((mp - 1,)), dma((mp - 1,)), dma((dp - 1,)), dma((dp - 1,)),
+            dma((dp - 1,)), dma((dp - 1,)), dma((mp - 1,)), dma((mp - 1,)),
+            dma((dp - 1,)), dma((dp - 1,)),
+        ],
+        compiler_params=pltpu.CompilerParams(
+            collective_id=2, has_side_effects=True, vmem_limit_bytes=24 << 20
+        ),
+    )(hid, ints, rewards, parts)
 
 
 def pick(mask, row):
@@ -242,24 +365,46 @@
     local_rows = table.shape[0]
     local_flat = hidden.reshape(own, width)
 
-    stacked = jnp.concatenate([local_flat, value_weight.reshape(1, width)], axis=0)
-    wide = lax.all_gather(stacked, "mp", axis=1, tiled=True)
-    flat, value_row = wide[:own], wide[own:]
-    values = (
-        jnp.sum(flat.astype(f32) * value_row.astype(f32), axis=1).reshape(prompts, slots)
-        + value_bias[0]
-    )
     positions = jnp.arange(slots, dtype=jnp.int32)[None, :]
-    follows = positions + 1 < lengths[:, None]
-    shifted = jnp.concatenate([values[:, 1:], jnp.zeros_like(values[:, :1])], axis=1)
-    target = rewards + discount * jnp.where(follows, shifted, 0.0)
-
-    ints = jnp.concatenate([actions, lengths[:, None]], axis=1)
-    all_ints = lax.all_gather(ints, "dp", axis=0, tiled=True)
-    all_lengths = all_ints[:, slots]
-    ids = all_ints[:, :slots].reshape(total)
-    facts = jnp.stack([target.reshape(own), values.reshape(own)])
-    all_facts = lax.all_gather(facts, "dp", axis=1, tiled=True)
+    mp = lax.axis_size("mp")
+    in_vmem = 30 * packed * cols < (32 << 20) and dp % mp == 0 and slots >= prompts
+    if in_vmem:
+        hid = jnp.transpose(local_flat.reshape(own, dp // mp, rows), (1, 0, 2))
+        part = jnp.sum(local_flat.astype(f32) * value_weight.astype(f32)[None, :], axis=1)
+        ints = jnp.zeros((8, own), jnp.int32)
+        ints = ints.at[0].set(actions.reshape(own)).at[1, :prompts].set(lengths)
+        pages, int_tiles, fact_tiles = spread_call(
+            dp, mp, hid, ints, jnp.broadcast_to(rewards.reshape(1, own), (8, own)),
+            jnp.broadcast_to(part[None, :], (8, own)),
+        )
+        spread = pages.reshape(total, rows)
+        ids = int_tiles[:, 0].reshape(total)
+        all_lengths = int_tiles[:, 1, :prompts].reshape(prompts * dp)
+        all_values = fact_tiles[:, 1].reshape(prompts * dp, slots) + value_bias[0]
+        all_rewards = fact_tiles[:, 0].reshape(prompts * dp, slots)
+        follows = positions + 1 < all_lengths[:, None]
+        shifted = jnp.concatenate([all_values[:, 1:], jnp.zeros_like(all_values[:, :1])], axis=1)
+        all_targets = all_rewards + discount * jnp.where(follows, shifted, 0.0)
+        all_facts = jnp.stack([all_targets.reshape(total), all_values.reshape(total)])
+    else:
+        stacked = jnp.concatenate([local_flat, value_weight.reshape(1, width)], axis=0)
+        wide = lax.all_gather(stacked, "mp", axis=1, tiled=True)
+        flat, value_row = wide[:own], wide[own:]
+        values = (
+            jnp.sum(flat.astype(f32) * value_row.astype(f32), axis=1).reshape(prompts, slots)
+            + value_bias[0]
+        )
+        follows = positions + 1 < lengths[:, None]
+        shifted = jnp.concatenate([values[:, 1:], jnp.zeros_like(values[:, :1])], axis=1)
+        target = rewards + discount * jnp.where(follows, shifted, 0.0)
+
+        ints = jnp.concatenate([actions, lengths[:, None]], axis=1)
+        all_ints = lax.all_gather(ints, "dp", axis=0, tiled=True)
+        all_lengths = all_ints[:, slots]
+        ids = all_ints[:, :slots].reshape(total)
+        facts = jnp.stack([target.reshape(own), values.reshape(own)])
+        all_facts = lax.all_gather(facts, "dp", axis=1, tiled=True)
+        spread = lax.all_to_all(flat, "dp", split_axis=1, concat_axis=0, tiled=True)
     count = jnp.sum(all_lengths).astype(f32)
     factor = 1.0 / count
 
@@ -289,14 +434,12 @@
     requests = pick(wanted, ids - me * local_rows)
     found = table[requests]
 
-    spread = lax.all_to_all(flat, "dp", split_axis=1, concat_axis=0, tiled=True)
     pack_mask = (jnp.arange(packed, dtype=jnp.int32)[:, None] == place[None, :]).astype(bf16)
     held = jnp.dot(pack_mask, spread, preferred_element_type=f32).astype(bf16)
 
     pack_bool = jnp.arange(packed, dtype=jnp.int32)[:, None] == place[None, :]
     goal = pick(pack_bool, all_facts[0])
     worth = pick(pack_bool, all_facts[1])
-    in_vmem = 30 * packed * cols < (32 << 20)
     if in_vmem:
         seats = pick(pack_bool, where_held) - me * own
         seat = (seats[:, None] == jnp.arange(own, dtype=jnp.int32)[None, :]).astype(bf16)

time: 207 us -> 184 us (0.89)
  blocking collectives: 53.9 us -> 0 us
  Pallas kernels: 115 us -> 151 us
  starting transfers between devices: 6.3 us -> 0 us
  local copies, waits for them, and re-layouts: 8.71 us -> 11.4 us
    all_gather x3 -> x0, blocking collectives: 53.9 us -> none  [the longest x1 30.9 us: on_device(): all_ints = lax.all_gather(ints, 'dp', axis=0, tiled=True)]
    pallas_call x0 -> x1, Pallas kernels: none -> 39.4 us  [spread_call(): pl.pallas_call(functools.partial(spread_kernel, dp, mp), out_shape=(jax.S...]
    all_to_all x1 -> x0, starting transfers between devices: 6.3 us -> none  [on_device(): spread = lax.all_to_all(flat, 'dp', split_axis=1, concat_axis=0, tiled=True)]
    pallas_call x1, Pallas kernels: 115 us -> 112 us  [reduce_call(): pl.pallas_call(functools.partial(reduce_kernel, dp, mp), out_shape=(jax.S...]
  transfers between devices with their start and end apart: 1 -> 0, of which waited for: 0 -> 0; matrix products, arithmetic and copies ran while one was open for 5% -> 0% of each run, Pallas kernels for 0% -> 0%
where the time goes in v3:
time: 184 us; the launch traced here: 183 us
  Pallas kernels  151 us (82%)
  local copies, waits for them, and re-layouts  11.4 us (6%)
  other arithmetic  8.91 us (5%)
  matrix products  6.4 us (3%)
  between operations  5.69 us (3%)
    pallas_call x1, Pallas kernels, reduce_call(): pl.pallas_call(functools.partial(reduce_kernel, dp, mp), out_shape=(jax.S...  112 us
    pallas_call x1, Pallas kernels, spread_call(): pl.pallas_call(functools.partial(spread_kernel, dp, mp), out_shape=(jax.S...  39.4 us

profile of v3, /device:TPU:16, one launch (start us, length us, event | category | flops | bytes accessed | tf_op | source)
XLA Modules:
  0.0 183.4 jit_solution(14891715521621206872)
XLA Ops:
  1.3 0.8 broadcast_in_dim.113
  2.0 0.8 reshape.267
  2.8 0.8 scatter.9.ints
  3.6 0.7 convert_element_type.39
  4.3 1.1 multiply_reduce_fusion
  5.4 0.1 broadcast_in_dim.115
  5.5 1.2 reshape_reshape.3
  6.7 39.4 %shard_map.162 = (bf16[8,128,448]{2,1,0:T(8,128)(2,1)S(1)}, s32[8,8,128]{2,1,0:T(8,128)S(1)}, f32[8,8,128]{2,1,0:T(8,128)S(1)}) custom-call(bf16[2,128,448]{2,1,0:T(8,128)(2,1)S(1)} %bitcast.35, s32[8,128]{1,0:T(8,128)S(1)} %scatter.9.ints, f32[8,128]{1,0:T(8,128)S(1)} %broadcast_in_dim.114.rewards, f32[8,128]{1,0:T(8,128)S(1)} %broadcast_in_dim.116.parts), custom_call_target="tpu_custom_call" | custom-call | tf_op jit(solution)/shard_map/pallas_call | solution.py:324
  46.2 0.6 slice_reduce_fusion.2
  47.5 0.1 lt.87
  47.6 0.1 select_reduce_fusion.4
  47.8 0.4 convert_reduce_fusion
  48.2 0.2 select_reduce_fusion.3
  48.6 1.5 fusion.1.held
  50.1 0.3 select_reduce_fusion.2
  50.4 0.5 broadcast.215
  50.9 0.7 fusion.13
  51.7 0.1 slice.87
  51.8 0.1 multiply_add_fusion
  52.0 0.7 select_reduce_fusion
  52.6 0.8 fusion.5.seat
  53.4 2.9 %gather_fusion = bf16[128,896]{1,0:T(8,128)(2,1)} fusion(bf16[19008,896]{1,0:T(8,128)(2,1)} %param.19, s32[1024]{0:T(1024)S(1)} %pad_clamp_fusion), kind=kCustom, calls=%fused_computation | custom fusion | bytes 459264 | tf_op jit(solution)/shard_map/gather | solution.py:435
  56.3 0.9 copy.26.goal
  57.2 0.9 copy.27.worth
  58.1 111.5 %shard_map.163 = (bf16[8,64,1792]{2,1,0:T(8,128)(2,1)}, f32[8,64,128]{2,1,0:T(8,128)}, f32[8,8,448]{2,1,0:T(8,128)}) custom-call(bf16[512,448]{1,0:T(8,128)(2,1)} %fusion.1.held, bf16[512,128]{1,0:T(8,128)(2,1)} %fusion.5.seat, bf16[128,896]{1,0:T(8,128)(2,1)} %gather_fusion, bf16[448,896]{1,0:T(8,128)(2,1)} %w_one.1, bf16[448,896]{1,0:T(8,128)(2,1)} %w_two.1, ...), custom_call_target="tpu_custom_call" | custom-call | tf_op jit(solution)/shard_map/pallas_call | solution.py:210
  169.6 1.2 copy.31
  170.8 0.6 fusion.9
  172.7 0.9 slice_reduce_fusion
  173.7 0.7 dynamic-slice_multiply_fusion
  174.4 3.1 %convolution_multiply_fusion = f32[448,896]{1,0:T(8,128)} fusion(bf16[512,448]{1,0:T(8,128)(2,1)S(1)} %copy-done, bf16[512,1792]{1,0:T(8,128)(2,1)} %bitcast.37, f32[]{:T(128)S(6)} %div.27), kind=kOutput, calls=%fused_computation.8 | convolution fusion | flops 411443200 | bytes 2981892 | tf_op jit(solution)/shard_map/dot_general | solution.py:501
  177.5 1.8 convolution_multiply_fusion.1
  179.3 1.8 add_convert_fusion
  (34 shorter events, 0.7 us)
Async XLA Ops:
  58.1 116.4 %copy-start = (bf16[512,448]{1,0:T(8,128)(2,1)S(1)}, bf16[512,448]{1,0:T(8,128)(2,1)}, u32[]{:S(2)}) copy-start(bf16[512,448]{1,0:T(8,128)(2,1)} %fusion.1.held) | copy-start | bytes 1376260
  169.6 7.9 %copy-start.5 = (bf16[8,64,1792]{2,1,0:T(8,128)(2,1)S(1)}, bf16[8,64,1792]{2,1,0:T(8,128)(2,1)}, u32[]{:S(2)}) copy-start(bf16[8,64,1792]{2,1,0:T(8,128)(2,1)} %get-tuple-element.41) | copy-start | bytes 5505028
  174.4 4.9 %copy-start.4 = (bf16[448,896]{1,0:T(8,128)(2,1)S(1)}, bf16[448,896]{1,0:T(8,128)(2,1)}, u32[]{:S(2)}) copy-start(bf16[448,896]{1,0:T(8,128)(2,1)} %w_four.1) | copy-start | bytes 2408452
  177.5 1.8 %copy-start.1 = (bf16[448,896]{1,0:T(8,128)(2,1)S(1)}, bf16[448,896]{1,0:T(8,128)(2,1)}, u32[]{:S(2)}) copy-start(bf16[448,896]{1,0:T(8,128)(2,1)} %w_one.1) | copy-start | bytes 2408452
  177.5 1.8 %copy-start.2 = (bf16[448,896]{1,0:T(8,128)(2,1)S(1)}, bf16[448,896]{1,0:T(8,128)(2,1)}, u32[]{:S(2)}) copy-start(bf16[448,896]{1,0:T(8,128)(2,1)} %w_two.1) | copy-start | bytes 2408452
  177.5 1.8 %copy-start.3 = (bf16[448,896]{1,0:T(8,128)(2,1)S(1)}, bf16[448,896]{1,0:T(8,128)(2,1)}, u32[]{:S(2)}) copy-start(bf16[448,896]{1,0:T(8,128)(2,1)} %w_three.1) | copy-start | bytes 2408452

commit v4 on v3

--- a/solution.py
+++ b/solution.py
@@ -293,18 +293,27 @@
         total = total + sums[r]
     row = lax.broadcasted_iota(jnp.int32, total.shape, 0)
     facts[me] = jnp.where(row == 0, rewards[...], total)
-    for copy in a_copies:
-        copy.wait()
-    b_copies = []
-    for r in range(1, dp):
-        to = lax.rem(me + r, dp)
-        b_copies.append(
-            send(wide.at[to], landed.at[me], b_send.at[r - 1], b_recv.at[r - 1], "dp", to)
-        )
     f_copies = [
         send(facts.at[me], facts.at[me], f_send.at[r - 1], f_recv.at[r - 1], "dp", lax.rem(me + r, dp))
         for r in range(1, dp)
     ]
+
+    def across(to, r):
+        return pltpu.make_async_remote_copy(
+            src_ref=wide.at[to], dst_ref=landed.at[me], send_sem=b_send.at[r - 1],
+            recv_sem=b_recv.at[r - 1], device_id={"dp": to}, device_id_type=MESH,
+        )
+
+    for step in range(mp):
+        if step > 0:
+            a_copies[step - 1].wait()
+        for q in range(per):
+            to = lax.rem(mine + mp - step, mp) * per + q
+
+            @pl.when(to != me)
+            def _():
+                across(to, lax.rem(to - me + dp, dp)).start()
+
     landed[me] = wide[me]
     for copy in i_copies:
         copy.wait()
@@ -312,8 +321,8 @@
     for copy in f_copies:
         copy.wait()
     float_out[...] = facts[...]
-    for copy in b_copies:
-        copy.wait()
+    for r in range(1, dp):
+        across(lax.rem(me + r, dp), r).wait()
     hid_out[...] = landed[...]
 
 

time: 184 us -> 176 us (0.957)
  Pallas kernels: 151 us -> 143 us
    pallas_call x1, Pallas kernels: 39.4 us -> 31.5 us  [spread_call(): pl.pallas_call(functools.partial(spread_kernel, dp, mp), out_shape=(jax.S...]
where the time goes in v4:
time: 176 us
  Pallas kernels  143 us (81%)
  local copies, waits for them, and re-layouts  11.4 us (6%)
  other arithmetic  8.91 us (5%)
  matrix products  6.41 us (4%)
  between operations  5.69 us (3%)
    pallas_call x1, Pallas kernels, reduce_call(): pl.pallas_call(functools.partial(reduce_kernel, dp, mp), out_shape=(jax.S...  112 us
    pallas_call x1, Pallas kernels, spread_call(): pl.pallas_call(functools.partial(spread_kernel, dp, mp), out_shape=(jax.S...  31.5 us

profile of v4, /device:TPU:16, one launch (start us, length us, event | category | flops | bytes accessed | tf_op | source)
XLA Modules:
  0.0 175.8 jit_solution(14443501640353738019)
XLA Ops:
  1.3 0.8 broadcast_in_dim.113
  2.0 0.8 reshape.267
  2.8 0.8 scatter.9.ints
  3.6 0.7 convert_element_type.39
  4.3 1.1 multiply_reduce_fusion
  5.4 0.1 broadcast_in_dim.115
  5.5 1.2 reshape_reshape.3
  6.7 31.5 %shard_map.162 = (bf16[8,128,448]{2,1,0:T(8,128)(2,1)S(1)}, s32[8,8,128]{2,1,0:T(8,128)S(1)}, f32[8,8,128]{2,1,0:T(8,128)S(1)}) custom-call(bf16[2,128,448]{2,1,0:T(8,128)(2,1)S(1)} %bitcast.35, s32[8,128]{1,0:T(8,128)S(1)} %scatter.9.ints, f32[8,128]{1,0:T(8,128)S(1)} %broadcast_in_dim.114.rewards, f32[8,128]{1,0:T(8,128)S(1)} %broadcast_in_dim.116.parts), custom_call_target="tpu_custom_call" | custom-call | tf_op jit(solution)/shard_map/pallas_call | solution.py:333
  38.2 0.6 slice_reduce_fusion.2
  39.6 0.1 lt.87
  39.6 0.1 select_reduce_fusion.4
  39.8 0.4 convert_reduce_fusion
  40.3 0.2 select_reduce_fusion.3
  40.7 1.5 fusion.1.held
  42.2 0.3 select_reduce_fusion.2
  42.5 0.5 broadcast.215
  43.0 0.7 fusion.13
  43.7 0.1 slice.87
  43.9 0.1 multiply_add_fusion
  44.0 0.7 select_reduce_fusion
  44.7 0.8 fusion.5.seat
  45.5 2.9 %gather_fusion = bf16[128,896]{1,0:T(8,128)(2,1)} fusion(bf16[19008,896]{1,0:T(8,128)(2,1)} %param.19, s32[1024]{0:T(1024)S(1)} %pad_clamp_fusion), kind=kCustom, calls=%fused_computation | custom fusion | bytes 459264 | tf_op jit(solution)/shard_map/gather | solution.py:444
  48.4 0.9 copy.26.goal
  49.3 0.9 copy.27.worth
  50.1 111.9 %shard_map.163 = (bf16[8,64,1792]{2,1,0:T(8,128)(2,1)}, f32[8,64,128]{2,1,0:T(8,128)}, f32[8,8,448]{2,1,0:T(8,128)}) custom-call(bf16[512,448]{1,0:T(8,128)(2,1)} %fusion.1.held, bf16[512,128]{1,0:T(8,128)(2,1)} %fusion.5.seat, bf16[128,896]{1,0:T(8,128)(2,1)} %gather_fusion, bf16[448,896]{1,0:T(8,128)(2,1)} %w_one.1, bf16[448,896]{1,0:T(8,128)(2,1)} %w_two.1, ...), custom_call_target="tpu_custom_call" | custom-call | tf_op jit(solution)/shard_map/pallas_call | solution.py:210
  162.0 1.2 copy.31
  163.2 0.6 fusion.9
  165.1 0.9 slice_reduce_fusion
  166.2 0.7 dynamic-slice_multiply_fusion
  166.8 3.1 %convolution_multiply_fusion = f32[448,896]{1,0:T(8,128)} fusion(bf16[512,448]{1,0:T(8,128)(2,1)S(1)} %copy-done, bf16[512,1792]{1,0:T(8,128)(2,1)} %bitcast.37, f32[]{:T(128)S(6)} %div.27), kind=kOutput, calls=%fused_computation.8 | convolution fusion | flops 411443200 | bytes 2981892 | tf_op jit(solution)/shard_map/dot_general | solution.py:510
  169.9 1.8 %convolution_multiply_fusion.1 = f32[448,896]{1,0:T(8,128)} fusion(bf16[512,448]{1,0:T(8,128)(2,1)S(1)} %copy-done, bf16[512,1792]{1,0:T(8,128)(2,1)S(1)} %bitcast.38, f32[]{:T(128)S(6)} %div.27), kind=kOutput, calls=%fused_computation.9 | convolution fusion | flops 411443200 | bytes 3047428 | tf_op jit(solution)/shard_map/dot_general | solution.py:507
  171.8 1.8 %add_convert_fusion = (bf16[448,896]{1,0:T(8,128)(2,1)}, bf16[448,896]{1,0:T(8,128)(2,1)}) fusion(bf16[448,896]{1,0:T(8,128)(2,1)S(1)} %copy-done.2, bf16[448,896]{1,0:T(8,128)(2,1)S(1)} %copy-done.4, bf16[448,896]{1,0:T(8,128)(2,1)S(1)} %copy-done.1, bf16[448,896]{1,0:T(8,128)(2,1)S(1)} %copy-done.3), kind=kLoop, calls=%fused_computation.6 | loop fusion | flops 4816896 | bytes 4816896 | tf_op jit(solution)/shard_map/convert_element_type | solution.py:528
  (34 shorter events, 0.7 us)
Async XLA Ops:
  50.1 116.7 %copy-start = (bf16[512,448]{1,0:T(8,128)(2,1)S(1)}, bf16[512,448]{1,0:T(8,128)(2,1)}, u32[]{:S(2)}) copy-start(bf16[512,448]{1,0:T(8,128)(2,1)} %fusion.1.held) | copy-start | bytes 1376260
  162.0 7.9 %copy-start.5 = (bf16[8,64,1792]{2,1,0:T(8,128)(2,1)S(1)}, bf16[8,64,1792]{2,1,0:T(8,128)(2,1)}, u32[]{:S(2)}) copy-start(bf16[8,64,1792]{2,1,0:T(8,128)(2,1)} %get-tuple-element.41) | copy-start | bytes 5505028
  166.8 4.9 %copy-start.4 = (bf16[448,896]{1,0:T(8,128)(2,1)S(1)}, bf16[448,896]{1,0:T(8,128)(2,1)}, u32[]{:S(2)}) copy-start(bf16[448,896]{1,0:T(8,128)(2,1)} %w_four.1) | copy-start | bytes 2408452
  169.9 1.8 %copy-start.1 = (bf16[448,896]{1,0:T(8,128)(2,1)S(1)}, bf16[448,896]{1,0:T(8,128)(2,1)}, u32[]{:S(2)}) copy-start(bf16[448,896]{1,0:T(8,128)(2,1)} %w_one.1) | copy-start | bytes 2408452
  169.9 1.8 %copy-start.2 = (bf16[448,896]{1,0:T(8,128)(2,1)S(1)}, bf16[448,896]{1,0:T(8,128)(2,1)}, u32[]{:S(2)}) copy-start(bf16[448,896]{1,0:T(8,128)(2,1)} %w_two.1) | copy-start | bytes 2408452
  169.9 1.8 %copy-start.3 = (bf16[448,896]{1,0:T(8,128)(2,1)S(1)}, bf16[448,896]{1,0:T(8,128)(2,1)}, u32[]{:S(2)}) copy-start(bf16[448,896]{1,0:T(8,128)(2,1)} %w_three.1) | copy-start | bytes 2408452
